TPU v7x, 256 devices: a whole 4x4x8 slice. The times are simulated.
256 devices in a mesh: facet: 16 (over y, x_hi, core), bl: 16 (over z, x_lo).
Axes of the slice: x: 4 (x_hi: 2, x_lo: 2; x = x_hi * 2 + x_lo), y: 4, z: 8, core: 2. Of those that a mesh axis runs over, the one named last changes fastest.
Arguments:
- facet_model: bfloat16 [16, 1024, 1024], P('facet', 'bl'), may hold values from -0.005859375 to 0.005859375
- screens: bfloat16 [16, 256, 64, 128], P('facet', 'bl'), may hold values from 0.099609375 to 1.8984375
- observed: float32 [192, 64, 128], P('bl'), may hold values from -24 to 24
- offsets: int32 [192, 2], P('bl'), may hold values from 0 to 4032
- stations: int32 [192, 2], P('bl'), may hold values from 0 to 255
- counts: int32 [16], P('bl'), may hold values from 1 to 12, as said below
Outputs:
- residual_vis: float32 [192, 64, 128], P('bl')
- residual_image: float32 [16, 1024, 1024], P('facet', 'bl')
Inputs may be any that keep to these rules, and one draw needn't show every extreme that they name: `counts`: some baseline block has all 12 slots live.
All inputs are finite; a program needn't handle non-finite values.
Results may differ from a plain program's by a relative error of at most 0.0061.
Values may be sent and summed in bfloat16 or wider, within the bound.
No kernel may reach another device: no remote copies, remote signals or barrier semaphores. Data moves between devices by JAX's collectives and lax.ppermute only.
A program may use at most 64 MiB of HBM per device.

v0:
```python
import math
import jax
import jax.numpy as jnp
from jax import lax
from jax.sharding import PartitionSpec as P

FGRID = 4


def tables(offset_u, offset_v, facet_id, tile_width, facet_cells):
    grid_cells = FGRID * facet_cells
    corner_x = facet_id // FGRID * facet_cells
    corner_y = facet_id % FGRID * facet_cells
    pixel_index = jnp.arange(facet_cells, dtype=jnp.int32)
    cell_index = jnp.arange(tile_width, dtype=jnp.int32)
    phase_u = jnp.mod(
        (offset_u + cell_index)[:, None] * (corner_x + pixel_index)[None, :], grid_cells
    )
    phase_v = jnp.mod(
        (offset_v + cell_index)[:, None] * (corner_y + pixel_index)[None, :], grid_cells
    )
    angle_u = phase_u.astype(jnp.float32) * (2.0 * math.pi / grid_cells)
    angle_v = phase_v.astype(jnp.float32) * (2.0 * math.pi / grid_cells)
    tab_u = jnp.concatenate([jnp.cos(angle_u), -jnp.sin(angle_u)], axis=0).astype(jnp.bfloat16)
    table_vertical = jnp.concatenate([jnp.cos(angle_v), jnp.sin(angle_v)], axis=0).astype(
        jnp.bfloat16
    )
    return (tab_u, table_vertical)


def half_splits(value):
    half_width = value.shape[-1] // 2
    return (value[..., :half_width], value[..., half_width:])


def complex_times(left_re, left_im, right_re, right_im):
    return (left_re * right_re - left_im * right_im, left_re * right_im + left_im * right_re)


def times_conj(left_re, left_im, right_re, right_im):
    return (left_re * right_re + left_im * right_im, left_im * right_re - left_re * right_im)


def per_device(facet_model, screens, observed, offsets, stations, counts):
    tile_count = observed.shape[0]
    tile_width = observed.shape[1]
    facet_cells = facet_model.shape[2]
    bl_devices = lax.axis_size("bl")
    facet_id = lax.axis_index("facet")
    make_tables = jax.vmap(tables, in_axes=(0, 0, None, None, None))
    tab_u, table_vertical = make_tables(
        offsets[:, 0], offsets[:, 1], facet_id, tile_width, facet_cells
    )
    upper_portion = jnp.einsum(
        "tkn,np->tkp",
        tab_u,
        lax.all_gather(facet_model[0], "bl", axis=0, tiled=True),
        preferred_element_type=jnp.float32,
    ).astype(jnp.bfloat16)
    block_groups = jnp.einsum(
        "gsf,gmf->gsm", upper_portion, table_vertical, preferred_element_type=jnp.float32
    )
    real_part = (
        block_groups[:, :tile_width, :tile_width] + block_groups[:, tile_width:, tile_width:]
    )
    imag_part = (
        block_groups[:, tile_width:, :tile_width] - block_groups[:, :tile_width, tile_width:]
    )
    all_screens = lax.all_gather(screens[0], "bl", axis=0, tiled=True)
    first_station_gain = jnp.take(all_screens, stations[:, 0], axis=0).astype(jnp.float32)
    gain_q = jnp.take(all_screens, stations[:, 1], axis=0).astype(jnp.float32)
    p_re, p_im = half_splits(first_station_gain)
    q_re, q_im = half_splits(gain_q)
    y_re, y_im = complex_times(p_re, p_im, real_part, imag_part)
    x_re, x_im = times_conj(y_re, y_im, q_re, q_im)
    contribution = jnp.concatenate([x_re, x_im], axis=2)
    live_mask = (jnp.arange(tile_count, dtype=jnp.int32) < counts[0])[:, None, None]
    predicted = lax.psum(contribution, "facet")
    residual = jnp.where(live_mask, observed - predicted, jnp.zeros_like(observed))
    r_re, r_im = half_splits(residual)
    z_re, z_im = times_conj(r_re, r_im, p_re, p_im)
    w_re, w_im = complex_times(z_re, z_im, q_re, q_im)
    w_re = w_re.astype(jnp.bfloat16)
    w_im = w_im.astype(jnp.bfloat16)
    stacked = jnp.concatenate(
        [jnp.concatenate([w_re, -w_im], axis=2), jnp.concatenate([w_im, w_re], axis=2)], axis=1
    )
    q_two = jnp.einsum(
        "tuk,tky->tuy", stacked, table_vertical, preferred_element_type=jnp.float32
    ).astype(jnp.bfloat16)
    image_scale = 1.0 / (32.0 * tile_width * math.sqrt(tile_count * bl_devices))
    row_count = facet_cells // bl_devices
    whole_image = jnp.einsum("tkx,tky->xy", tab_u, q_two, preferred_element_type=jnp.float32)
    summed = lax.psum(whole_image, "bl")
    own_rows = lax.dynamic_slice_in_dim(summed, lax.axis_index("bl") * row_count, row_count, 0)
    residual_image = (own_rows * image_scale)[None]
    return (residual, residual_image)


def solution(mesh):
    in_specs = (
        P("facet", "bl", None),
        P("facet", "bl", None, None),
        P("bl", None, None),
        P("bl", None),
        P("bl", None),
        P("bl"),
    )
    out_specs = (P("bl", None, None), P("facet", "bl", None))
    return jax.shard_map(
        per_device, mesh=mesh, in_specs=in_specs, out_specs=out_specs, check_vma=False
    )
```

profile of v0, /device:TPU:16, one launch (start us, length us, event | category | flops | bytes accessed | tf_op | source)
XLA Modules:
  0.0 557.0 jit_solution(6302353294279317188)
XLA Ops:
  7.2 0.0 all-gather.7.cloned.1.call-start
  7.2 0.7 all-gather.7.cloned.1.call-update
  7.9 0.0 all-gather.5.cloned.1.call-start
  7.9 0.7 all-gather.5.cloned.1.call-update
  8.6 0.0 all-reduce.3.cloned.1.call-start
  8.7 0.8 compare_and_fusion.1
  9.5 0.8 slice_bitcast_fusion.1
  10.3 0.1 iota_add_fusion
  10.4 14.1 %cosine_convert_fusion = (bf16[12,64,1024]{2,1,0:T(8,128)(2,1)S(1)}, bf16[12,64,1024]{2,1,0:T(8,128)(2,1)}) fusion(s32[1024]{0:T(1024)S(1)} %iota_add_fusion.2, s32[12,64]{1,0:T(8,128)S(1)} %get-tuple-element.24), kind=kLoop, calls=%fused_computation.23 | loop fusion | flops 12582912 | bytes 3152896 | tf_op jit(solution)/shard_map/convert
  24.4 14.2 %cosine_convert_fusion.1 = (bf16[12,64,1024]{2,1,0:T(8,128)(2,1)}, bf16[12,64,1024]{2,1,0:T(8,128)(2,1)}) fusion(s32[1024]{0:T(1024)S(1)} %iota_add_fusion.3, s32[12,64]{1,0:T(8,128)S(1)} %get-tuple-element.25), kind=kLoop, calls=%fused_computation.27 | loop fusion | flops 13369344 | bytes 3152896 | tf_op jit(solution)/shard_map/convert.2
  38.7 46.7 %all-gather.7.cloned.1.call-done = bf16[1,1024,1024]{2,1,0:T(8,128)(2,1)} async-done(((bf16[1,64,1024]{2,1,0:T(8,128)(2,1)}), bf16[1,1024,1024]{2,1,0:T(8,128)(2,1)}) %all-gather.7.cloned.1.call-update) | async-done | bytes 2097168 | tf_op jit(solution)/shard_map/all_gather | solution.py:57
  85.4 7.2 %fusion.8 = f32[12,128,128]{2,1,0:T(8,128)S(1)} fusion(bf16[12,64,1024]{2,1,0:T(8,128)(2,1)} %get-tuple-element.17, bf16[12,64,1024]{2,1,0:T(8,128)(2,1)S(1)} %get-tuple-element.16, bf16[1,1024,1024]{2,1,0:T(8,128)(2,1)} %all-gather.7.cloned.1.call-done, bf16[12,64,1024]{2,1,0:T(8,128)(2,1)} %get-tuple-element.15, bf16[12,64,1024]{2,1,0:T(8,128)(2,1)} %get-tuple-element.14), kind=kOutput, calls=%fused_computation.24 | convolution fusion | flops 3638034432 | bytes 9175040 | tf_op jit(solution)/shard_map/gsf,gmf->gsm/dot_general | solution.py:60
  92.6 92.0 %all-gather.5.cloned.1.call-done = bf16[1,256,64,128]{3,2,0,1:T(8,128)(2,1)} async-done(((bf16[1,16,64,128]{3,2,0,1:T(8,128)(2,1)}), bf16[1,256,64,128]{3,2,0,1:T(8,128)(2,1)}) %all-gather.5.cloned.1.call-update) | async-done | bytes 4194320 | tf_op jit(solution)/shard_map/all_gather | solution.py:69
  184.6 2.8 gather_fusion.1
  187.4 2.8 gather_fusion
  190.1 0.1 select_convert_fusion
  190.3 0.0 copy-start.1
  190.3 0.5 multiply_add_fusion.1
  190.8 0.2 multiply_subtract_fusion.1
  191.0 0.9 pad_maximum_fusion.11
  191.9 0.0 all-reduce.3.cloned.1.call-update
  191.9 0.2 all-reduce.5.cloned.1.call-start
  192.8 134.5 %all-reduce.3.cloned.1.call-done = f32[12,64,128]{2,1,0:T(8,128)} async-done(((f32[12,64,128]{2,1,0:T(8,128)}), f32[12,64,128]{2,1,0:T(8,128)}) %all-reduce.3.cloned.1.call-update) | async-done | bytes 393232 | tf_op jit(solution)/shard_map/psum | solution.py:78
  327.3 0.0 copy-done.1
  327.3 1.1 subtract_select_fusion
  328.4 0.0 copy-start
  328.4 0.4 fusion.39
  328.8 0.2 subtract_convert_fusion
  329.0 8.6 %fusion.12 = f32[1024,1024]{1,0:T(8,128)} fusion(bf16[12,64,1024]{2,1,0:T(8,128)(2,1)} %get-tuple-element.17, bf16[12,64,1024]{2,1,0:T(8,128)(2,1)S(1)} %get-tuple-element.16, bf16[12,64,1024]{2,1,0:T(8,128)(2,1)} %get-tuple-element.15, bf16[12,64,1024]{2,1,0:T(8,128)(2,1)} %get-tuple-element.14, bf16[12,64,64]{2,1,0:T(8,128)(2,1)S(1)} %subtract_convert_fusion, ...), kind=kOutput, calls=%fused_computation.29 | convolution fusion | flops 3639607296 | bytes 10780672 | tf_op jit(solution)/shard_map/tkx,tky->xy/dot_general | solution.py:93
  337.6 0.0 copy-done
  337.6 0.0 all-reduce.5.cloned.1.call-update
  337.7 211.1 %all-reduce.5.cloned.1.call-done = f32[1024,1024]{1,0:T(8,128)} async-done(((f32[1024,1024]{1,0:T(8,128)}), f32[1024,1024]{1,0:T(8,128)}) %all-reduce.5.cloned.1.call-update) | async-done | bytes 4194320 | tf_op jit(solution)/shard_map/psum | solution.py:94
  548.8 1.7 multiply_bitcast_fusion
  (5 shorter events, 0.0 us)
Async XLA Ops:
  7.2 78.2 %all-gather.7.cloned.1.call-start = ((), (), s32[]{:S(2)}) async-start(), calls=%async_computation.3 | async-start | bytes 2228224 | tf_op jit(solution)/shard_map/all_gather | solution.py:57
  7.9 176.7 %all-gather.5.cloned.1.call-start = ((), (), s32[]{:S(2)}) async-start(), calls=%async_computation.2 | async-start | bytes 4456448 | tf_op jit(solution)/shard_map/all_gather | solution.py:69
  8.6 318.6 %all-reduce.3.cloned.1.call-start = ((), (), s32[]{:S(2)}) async-start(), calls=%async_computation | async-start | bytes 786432 | tf_op jit(solution)/shard_map/psum | solution.py:78
  190.3 137.0 %copy-start.1 = (f32[12,64,128]{2,1,0:T(8,128)S(1)}, f32[12,64,128]{2,1,0:T(8,128)}, u32[]{:S(2)}) copy-start(f32[12,64,128]{2,1,0:T(8,128)} %param.10) | copy-start | bytes 1179652
  191.9 356.9 %all-reduce.5.cloned.1.call-start = ((), (), s32[]{:S(2)}) async-start(), calls=%async_computation.1 | async-start | bytes 8388608 | tf_op jit(solution)/shard_map/psum | solution.py:94
  328.4 9.2 %copy-start = (f32[12,64,128]{2,1,0:T(8,128)}, f32[12,64,128]{2,1,0:T(8,128)S(1)}, u32[]{:S(2)}) copy-start(f32[12,64,128]{2,1,0:T(8,128)S(1)} %subtract_select_fusion) | copy-start | bytes 1179652
Sparse Core Ops, SparseCore 0:
  9.8 75.5 all-gather.6
  87.2 97.3 all-gather.4
  192.0 135.2 all-reduce.2
  337.8 210.9 all-reduce.4
where the time goes:
time: 557 us
  waiting for transfers between devices  486 us (87%)
  other arithmetic  34.2 us (6%)
  matrix products  15.9 us (3%)
  between operations  14.6 us (3%)
  local copies, waits for them, and re-layouts  6.31 us (1%)
    psum x1, waiting for transfers between devices, per_device(): summed = lax.psum(whole_image, 'bl')  211 us
    psum x1, waiting for transfers between devices, per_device(): predicted = lax.psum(contribution, 'facet')  134 us
    all_gather x1, waiting for transfers between devices, per_device(): all_screens = lax.all_gather(screens[0], 'bl', axis=0, tiled=True)  92 us
    all_gather x1, waiting for transfers between devices, per_device(): lax.all_gather(facet_model[0], 'bl', axis=0, tiled=True)  46.7 us
    another operation x2, other arithmetic  28.3 us
  transfers between devices with their start and end apart: 4, of which 4 were waited for; matrix products, arithmetic and copies ran while one was open for 7% of the time, Pallas kernels for 0%

commit v1 on v0

--- a/solution.py
+++ b/solution.py
@@ -54,7 +54,9 @@
     upper_portion = jnp.einsum(
         "tkn,np->tkp",
         tab_u,
-        lax.all_gather(facet_model[0], "bl", axis=0, tiled=True),
+        jnp.concatenate(
+            lax.all_to_all(jnp.stack([facet_model[0]] * lax.axis_size("bl")), "bl", 0, 0), axis=0
+        ),
         preferred_element_type=jnp.float32,
     ).astype(jnp.bfloat16)
     block_groups = jnp.einsum(

time: 557 us -> 515 us (0.925)
  waiting for transfers between devices: 486 us -> 431 us
  starting transfers between devices: 0.34 us -> 9.8 us
    all_gather x1 -> x0, waiting for transfers between devices: 46.7 us -> none  [per_device(): lax.all_gather(facet_model[0], 'bl', axis=0, tiled=True)]
    all_gather x1, waiting for transfers between devices: 92 us -> 54.8 us  [per_device(): all_screens = lax.all_gather(screens[0], 'bl', axis=0, tiled=True)]
    all_to_all x0 -> x1, waiting for transfers between devices: none -> 31.5 us  [per_device(): lax.all_to_all(jnp.stack([facet_model[0]] * lax.axis_size('bl')), 'bl', 0...]
    all_to_all x0 -> x1, starting transfers between devices: none -> 9.5 us  [per_device(): lax.all_to_all(jnp.stack([facet_model[0]] * lax.axis_size('bl')), 'bl', 0...]
  transfers between devices with their start and end apart: 4 -> 4, of which waited for: 4 -> 4; matrix products, arithmetic and copies ran while one was open for 7% -> 8% of each run, Pallas kernels for 0% -> 0%
where the time goes in v1:
time: 515 us
  waiting for transfers between devices  431 us (84%)
  other arithmetic  33.6 us (7%)
  matrix products  16.3 us (3%)
  between operations  14.6 us (3%)
  starting transfers between devices  9.8 us (2%)
  local copies, waits for them, and re-layouts  9.47 us (2%)
    psum x1, waiting for transfers between devices, per_device(): summed = lax.psum(whole_image, 'bl')  211 us
    psum x1, waiting for transfers between devices, per_device(): predicted = lax.psum(contribution, 'facet')  133 us
    all_gather x1, waiting for transfers between devices, per_device(): all_screens = lax.all_gather(screens[0], 'bl', axis=0, tiled=True)  54.8 us
    all_to_all x1, waiting for transfers between devices, per_device(): lax.all_to_all(jnp.stack([facet_model[0]] * lax.axis_size('bl')), 'bl', 0...  31.5 us
    another operation x2, other arithmetic  28.4 us
  transfers between devices with their start and end apart: 4, of which 4 were waited for; matrix products, arithmetic and copies ran while one was open for 8% of the time, Pallas kernels for 0%

profile of v1, /device:TPU:16, one launch (start us, length us, event | category | flops | bytes accessed | tf_op | source)
XLA Modules:
  0.0 515.0 jit_solution(2448831931276313944)
XLA Ops:
  7.2 0.0 all-gather.3.cloned.1.call-start
  7.2 0.7 all-gather.3.cloned.1.call-update
  7.9 0.0 copy-start.4
  7.9 0.0 copy-start.5
  7.9 2.5 stack.3
  10.5 9.5 %all-to-all-start = ((bf16[16,64,1024]{2,1,0:T(8,128)(2,1)}), bf16[16,64,1024]{2,1,0:T(8,128)(2,1)S(1)}, u32[]{:S(2)}, u32[]{:S(2)}) async-start(bf16[16,64,1024]{2,1,0:T(8,128)(2,1)} %stack.3), calls=%async_computation | async-start | bytes 4194304 | tf_op jit(solution)/shard_map/all_to_all | solution.py:58
  20.0 0.0 all-reduce.3.cloned.1.call-start
  20.1 0.0 copy-done.4
  20.1 0.0 copy-done.5
  20.1 0.1 iota_add_fusion
  20.2 14.1 %cosine_convert_fusion = (bf16[12,64,1024]{2,1,0:T(8,128)(2,1)}, bf16[12,64,1024]{2,1,0:T(8,128)(2,1)}) fusion(s32[1024]{0:T(1024)S(1)} %iota_add_fusion.2, s32[12,64]{1,0:T(8,128)S(1)} %get-tuple-element.24), kind=kLoop, calls=%fused_computation.23 | loop fusion | flops 12582912 | bytes 3152896 | tf_op jit(solution)/shard_map/convert
  34.3 14.2 %cosine_convert_fusion.1 = (bf16[12,64,1024]{2,1,0:T(8,128)(2,1)}, bf16[12,64,1024]{2,1,0:T(8,128)(2,1)}) fusion(s32[1024]{0:T(1024)S(1)} %iota_add_fusion.3, s32[12,64]{1,0:T(8,128)S(1)} %get-tuple-element.25), kind=kLoop, calls=%fused_computation.27 | loop fusion | flops 13369344 | bytes 3152896 | tf_op jit(solution)/shard_map/convert.2
  48.5 31.5 %all-to-all-done = bf16[16,64,1024]{2,1,0:T(8,128)(2,1)S(1)} async-done(((bf16[16,64,1024]{2,1,0:T(8,128)(2,1)}), bf16[16,64,1024]{2,1,0:T(8,128)(2,1)S(1)}, u32[]{:S(2)}, u32[]{:S(2)}) %all-to-all-start) | async-done | bytes 2097184 | tf_op jit(solution)/shard_map/all_to_all | solution.py:58
  80.0 0.0 copy-start.1
  80.0 1.4 copy-done.1
  81.4 7.7 %fusion.8 = f32[12,128,128]{2,1,0:T(8,128)S(1)} fusion(bf16[12,64,1024]{2,1,0:T(8,128)(2,1)} %get-tuple-element.17, bf16[12,64,1024]{2,1,0:T(8,128)(2,1)} %get-tuple-element.16, bf16[1024,1024,1]{1,0,2:T(8,128)(2,1)} %bitcast.23, bf16[12,64,1024]{2,1,0:T(8,128)(2,1)} %get-tuple-element.15, bf16[12,64,1024]{2,1,0:T(8,128)(2,1)} %get-tuple-element.14), kind=kOutput, calls=%fused_computation.24 | convolution fusion | flops 3638034432 | bytes 9175040 | tf_op jit(solution)/shard_map/gsf,gmf->gsm/dot_general | solution.py:62
  89.1 54.8 %all-gather.3.cloned.1.call-done = bf16[1,256,64,128]{3,2,0,1:T(8,128)(2,1)} async-done(((bf16[1,16,64,128]{3,2,0,1:T(8,128)(2,1)}), bf16[1,256,64,128]{3,2,0,1:T(8,128)(2,1)}) %all-gather.3.cloned.1.call-update) | async-done | bytes 4194320 | tf_op jit(solution)/shard_map/all_gather | solution.py:71
  143.9 2.8 gather_fusion.1
  146.6 2.8 gather_fusion
  149.4 0.1 select_convert_fusion
  149.5 0.1 select_convert_fusion.1
  149.6 0.0 copy-start.3
  149.7 0.5 multiply_add_fusion.1
  150.1 0.2 multiply_subtract_fusion.1
  150.3 0.9 pad_maximum_fusion.11
  151.2 0.0 all-reduce.3.cloned.1.call-update
  151.3 0.2 all-reduce.5.cloned.1.call-start
  152.2 0.0 copy-start.2
  152.2 133.3 %all-reduce.3.cloned.1.call-done = f32[12,64,128]{2,1,0:T(8,128)} async-done(((f32[12,64,128]{2,1,0:T(8,128)}), f32[12,64,128]{2,1,0:T(8,128)}) %all-reduce.3.cloned.1.call-update) | async-done | bytes 393232 | tf_op jit(solution)/shard_map/psum | solution.py:80
  285.4 0.0 copy-done.3
  285.4 1.1 subtract_select_fusion
  286.6 0.0 copy-start
  286.6 0.4 fusion.34
  286.9 0.2 subtract_convert_fusion
  287.1 0.0 copy-done.2
  287.2 8.6 %fusion.12 = f32[1024,1024]{1,0:T(8,128)} fusion(bf16[12,64,1024]{2,1,0:T(8,128)(2,1)} %get-tuple-element.17, bf16[12,64,1024]{2,1,0:T(8,128)(2,1)S(1)} %copy-done.2, bf16[12,64,1024]{2,1,0:T(8,128)(2,1)} %get-tuple-element.15, bf16[12,64,1024]{2,1,0:T(8,128)(2,1)} %get-tuple-element.14, bf16[12,64,64]{2,1,0:T(8,128)(2,1)S(1)} %subtract_convert_fusion, ...), kind=kOutput, calls=%fused_computation.29 | convolution fusion | flops 3639607296 | bytes 10780672 | tf_op jit(solution)/shard_map/tkx,tky->xy/dot_general | solution.py:95
  295.8 0.0 copy-done
  295.8 0.0 all-reduce.5.cloned.1.call-update
  295.8 211.0 %all-reduce.5.cloned.1.call-done = f32[1024,1024]{1,0:T(8,128)} async-done(((f32[1024,1024]{1,0:T(8,128)}), f32[1024,1024]{1,0:T(8,128)}) %all-reduce.5.cloned.1.call-update) | async-done | bytes 4194320 | tf_op jit(solution)/shard_map/psum | solution.py:96
  506.8 1.7 multiply_bitcast_fusion
  (6 shorter events, 0.0 us)
Async XLA Ops:
  7.2 136.7 %all-gather.3.cloned.1.call-start = ((), (), s32[]{:S(2)}) async-start(), calls=%async_computation.3 | async-start | bytes 4456448 | tf_op jit(solution)/shard_map/all_gather | solution.py:71
  7.9 12.2 %copy-start.4 = (s32[12,2]{0,1:T(2,128)S(1)}, s32[12,2]{0,1:T(2,128)}, u32[]{:S(2)}) copy-start(s32[12,2]{0,1:T(2,128)} %param.12) | copy-start | bytes 292
  7.9 12.2 %copy-start.5 = (s32[12,2]{0,1:T(2,128)S(1)}, s32[12,2]{0,1:T(2,128)}, u32[]{:S(2)}) copy-start(s32[12,2]{0,1:T(2,128)} %param.11) | copy-start | bytes 292
  10.5 69.5 %all-to-all-start = ((bf16[16,64,1024]{2,1,0:T(8,128)(2,1)}), bf16[16,64,1024]{2,1,0:T(8,128)(2,1)S(1)}, u32[]{:S(2)}, u32[]{:S(2)}) async-start(bf16[16,64,1024]{2,1,0:T(8,128)(2,1)} %stack.3), calls=%async_computation | async-start | bytes 4194304 | tf_op jit(solution)/shard_map/all_to_all | solution.py:58
  20.0 265.5 %all-reduce.3.cloned.1.call-start = ((), (), s32[]{:S(2)}) async-start(), calls=%async_computation.1 | async-start | bytes 786432 | tf_op jit(solution)/shard_map/psum | solution.py:80
  80.0 1.4 copy-start.1
  149.6 135.8 %copy-start.3 = (f32[12,64,128]{2,1,0:T(8,128)S(1)}, f32[12,64,128]{2,1,0:T(8,128)}, u32[]{:S(2)}) copy-start(f32[12,64,128]{2,1,0:T(8,128)} %param.10) | copy-start | bytes 1179652
  151.3 355.6 %all-reduce.5.cloned.1.call-start = ((), (), s32[]{:S(2)}) async-start(), calls=%async_computation.2 | async-start | bytes 8388608 | tf_op jit(solution)/shard_map/psum | solution.py:96
  152.2 135.0 %copy-start.2 = (bf16[12,64,1024]{2,1,0:T(8,128)(2,1)S(1)}, bf16[12,64,1024]{2,1,0:T(8,128)(2,1)}, u32[]{:S(2)}) copy-start(bf16[12,64,1024]{2,1,0:T(8,128)(2,1)} %get-tuple-element.16) | copy-start | bytes 4718596
  286.6 9.2 %copy-start = (f32[12,64,128]{2,1,0:T(8,128)}, f32[12,64,128]{2,1,0:T(8,128)S(1)}, u32[]{:S(2)}) copy-start(f32[12,64,128]{2,1,0:T(8,128)S(1)} %subtract_select_fusion) | copy-start | bytes 1179652
Sparse Core Ops, SparseCore 0:
  9.8 134.0 all-gather.2
  151.4 134.0 all-reduce.2
  295.9 210.8 all-reduce.4
